TPU v7x, 32 devices: a whole 2x2x4 slice. The times are simulated.
32 devices in a mesh: dp: 8 (over y, x, core), own: 4 (over z).
Axes of the slice: x: 2, y: 2, z: 4, core: 2. Of those that a mesh axis runs over, the one named last changes fastest.
Arguments:
- grads: bfloat16 [8, 6, 8192, 128], P('dp', None, 'own'), may hold values from -6 to 6
- proj: bfloat16 [4, 3, 8192, 1024], P('own', None, 'dp'), may hold values from -0.0625 to 0.0625
- moment1: float32 [4, 3, 1024, 128], P('own', None, 'dp'), may hold values from -24 to 24
- moment2: float32 [4, 3, 1024, 128], P('own', None, 'dp'), may hold values from 0.05 to 5
- plan: int32 [6], replicated, may hold values from 0 to 3, as said below
Outputs:
- update: bfloat16 [6, 8192, 128], P(None, 'own')
- new_moment1: float32 [4, 3, 1024, 128], P('own', None, 'dp')
- new_moment2: float32 [4, 3, 1024, 128], P('own', None, 'dp')
Inputs may be any that keep to these rules, and one draw needn't show every extreme that they name: `plan`: no owner is named more than 3 times, and some owner is named exactly 3 times.
All inputs are finite; a program needn't handle non-finite values.
Results may differ from a plain program's by a relative error of at most 0.015.
Values may be sent and summed in bfloat16 or wider, within the bound.
A program may use at most 64 MiB of HBM per device.

v0:
```python
import jax
import jax.numpy as jnp
from jax import lax
from jax.sharding import PartitionSpec as P

beta_one = 0.9
beta_two = 0.999
adam_eps = 1e-08
norm_eps = 1e-06
correct_one = 1.0 - 0.9**10
correct_two = 1.0 - 0.999**10


def slot_selector(plan, owner_count, capacity):
    matrices = plan.shape[0]
    places = jnp.arange(owner_count * capacity, dtype=jnp.int32)
    owners = places // capacity
    within = places % capacity
    index = jnp.arange(matrices, dtype=jnp.int32)
    before = jnp.sum(
        ((plan[None, :] == plan[:, None]) & (index[None, :] < index[:, None])).astype(jnp.int32),
        axis=1,
    )
    chosen = (plan[None, :] == owners[:, None]) & (before[None, :] == within[:, None])
    return chosen.astype(jnp.bfloat16)


def adam_moments(rank_share, first_old, second_old):
    first_new = beta_one * first_old + (1.0 - beta_one) * rank_share
    second_new = beta_two * second_old + (1.0 - beta_two) * rank_share * rank_share
    adam_step = first_new / correct_one / (jnp.sqrt(second_new / correct_two) + adam_eps)
    return (first_new, second_new, adam_step.astype(jnp.bfloat16))


def local(grads, proj, moment1, moment2, plan):
    owner_count = lax.axis_size("own")
    replica_count = lax.axis_size("dp")
    capacity = proj.shape[1]
    own_rows = grads.shape[2]
    columns = grads.shape[3]
    rank_rows = moment1.shape[2]
    selector = slot_selector(plan, owner_count, capacity)
    outgoing = jnp.einsum(
        "sj,jdc->sdc", selector, grads[0], preferred_element_type=jnp.float32
    ).astype(jnp.bfloat16)
    group_ratio = replica_count // owner_count
    piece_rows = own_rows // replica_count
    blocked = outgoing.reshape(owner_count * capacity, replica_count, piece_rows, columns)
    pieces = lax.psum_scatter(blocked, "dp", scatter_dimension=1, tiled=True).astype(jnp.float32)
    pieces = pieces.reshape(owner_count, capacity, piece_rows, columns)
    routed = lax.all_to_all(
        pieces.astype(jnp.bfloat16), "own", split_axis=0, concat_axis=0, tiled=True
    ).astype(pieces.dtype)
    span_pos = lax.axis_index("dp") // owner_count
    marker = (jnp.arange(group_ratio, dtype=jnp.int32) == span_pos).astype(jnp.float32)
    placed = routed[:, None] * marker[None, :, None, None, None]
    placed = placed.reshape(replica_count, capacity, piece_rows, columns)
    received = lax.all_to_all(
        placed.astype(jnp.bfloat16), "dp", split_axis=0, concat_axis=0, tiled=True
    ).astype(placed.dtype)
    received = received.reshape(group_ratio, owner_count, capacity, piece_rows, columns)
    mine = lax.axis_index("dp") % group_ratio
    kept = lax.dynamic_index_in_dim(received, mine, 0, keepdims=False)
    summed = jnp.transpose(kept, (1, 0, 2, 3)).reshape(capacity, owner_count * piece_rows, columns)
    grad_half = summed.astype(jnp.bfloat16)
    projection = proj[0]
    partial_value = jnp.einsum(
        "kdr,kdc->krc", projection, grad_half, preferred_element_type=jnp.float32
    )
    first_old = moment1[0]
    second_old = moment2[0]
    rank_full = lax.psum(partial_value.astype(jnp.bfloat16), "dp").astype(jnp.float32)
    rank_start = lax.axis_index("dp") * rank_rows
    rank_share = lax.dynamic_slice_in_dim(rank_full, rank_start, rank_rows, 1)
    first_new, second_new, adam_half = adam_moments(rank_share, first_old, second_old)
    adam_full = lax.all_gather(adam_half, "dp", axis=1, tiled=True)
    rank_half = rank_full.astype(jnp.bfloat16)
    grad_norms = jnp.sum(rank_full * rank_full, axis=1)
    adam_wide = adam_full.astype(jnp.float32)
    step_norms = jnp.sum(adam_wide * adam_wide, axis=1)
    column_scale = jnp.sqrt(step_norms) / (jnp.sqrt(grad_norms) + norm_eps)
    combined = (adam_wide - column_scale[:, None, :] * rank_half.astype(jnp.float32)).astype(
        jnp.bfloat16
    )
    update_full = (
        jnp.einsum("kdr,krc->kdc", projection, combined, preferred_element_type=jnp.float32)
        + column_scale[:, None, :] * summed
    )
    update_half = update_full.astype(jnp.bfloat16)
    gathered = lax.all_gather(update_half, "dp", axis=1, tiled=True)
    gathered = gathered.reshape(capacity, owner_count, own_rows, columns)
    returned = lax.all_to_all(gathered, "own", split_axis=1, concat_axis=0, tiled=True)
    slot_rows = returned.reshape(owner_count * capacity, own_rows, columns)
    update = jnp.einsum(
        "sj,sdc->jdc", selector, slot_rows, preferred_element_type=jnp.float32
    ).astype(jnp.bfloat16)
    return (update, first_new[None], second_new[None])


def solution(mesh):
    return jax.shard_map(
        local,
        mesh=mesh,
        in_specs=(
            P("dp", None, "own", None),
            P("own", None, "dp", None),
            P("own", None, "dp", None),
            P("own", None, "dp", None),
            P(),
        ),
        out_specs=(P(None, "own", None), P("own", None, "dp", None), P("own", None, "dp", None)),
        check_vma=False,
    )
```

profile of v0, /device:TPU:0, one launch (start us, length us, event | category | flops | bytes accessed | tf_op | source)
XLA Modules:
  0.0 447.2 jit_solution(17571062850924733432)
XLA Ops:
  7.2 1.0 convert_reduce_fusion
  8.2 0.8 copy-done
  9.1 13.2 %convolution_convert_fusion = bf16[12,2048,128]{2,0,1:T(8,128)(2,1)S(1)} fusion(bf16[6,2048,128]{2,1,0:T(8,128)(2,1)S(1)} %bitcast.60, s32[12]{0:T(128)S(1)} %get-tuple-element.18, s32[12]{0:T(128)S(1)} %get-tuple-element.19, s32[6]{0:T(128)S(1)} %convert_reduce_fusion, s32[6]{0:T(128)} %param.9), kind=kOutput, calls=%fused_computation.2 | convolution fusion | flops 40894680 | bytes 9437328 | tf_op jit(solution)/shard_map/sj,jdc->sdc/dot_general | solution.py:43
  22.3 4.4 copy.37
  26.8 64.6 %reduce-scatter.2.cloned.1.call-done = bf16[12,1,256,128]{3,2,0,1:T(8,128)(2,1)} async-done(((bf16[12,8,256,128]{3,2,0,1:T(8,128)(2,1)}), bf16[12,1,256,128]{3,2,0,1:T(8,128)(2,1)}) %reduce-scatter.2.cloned.1.call-update) | async-done | bytes 786448 | tf_op jit(solution)/shard_map/reduce_scatter | solution.py:49
  91.4 4.6 %all-to-all-start = ((bf16[4,3,256,128]{3,2,1,0:T(8,128)(2,1)}), bf16[4,3,256,128]{3,2,1,0:T(8,128)(2,1)S(1)}, u32[]{:S(2)}, u32[]{:S(2)}) async-start(bf16[4,3,256,128]{3,2,1,0:T(8,128)(2,1)} %bitcast.63), calls=%async_computation.1 | async-start | bytes 1572864 | tf_op jit(solution)/shard_map/all_to_all | solution.py:51
  96.1 19.8 %all-to-all-done = bf16[4,3,256,128]{3,2,1,0:T(8,128)(2,1)S(1)} async-done(((bf16[4,3,256,128]{3,2,1,0:T(8,128)(2,1)}), bf16[4,3,256,128]{3,2,1,0:T(8,128)(2,1)S(1)}, u32[]{:S(2)}, u32[]{:S(2)}) %all-to-all-start) | async-done | bytes 786464 | tf_op jit(solution)/shard_map/all_to_all | solution.py:51
  116.0 0.1 convert_element_type.58
  116.1 1.6 fusion.7
  117.7 3.6 all-to-all-start.1
  121.3 20.9 %all-to-all-done.1 = bf16[8,3,256,128]{3,2,1,0:T(8,128)(2,1)S(1)} async-done(((bf16[8,3,256,128]{3,2,1,0:T(8,128)(2,1)}), bf16[8,3,256,128]{3,2,1,0:T(8,128)(2,1)S(1)}, u32[]{:S(2)}, u32[]{:S(2)}) %all-to-all-start.1) | async-done | bytes 1572896 | tf_op jit(solution)/shard_map/all_to_all | solution.py:58
  142.2 0.1 convert_bitcast_fusion
  142.4 0.8 copy.38
  143.2 0.8 reshape.73
  144.0 4.7 %fusion.19 = bf16[3,1024,128]{1,2,0:T(8,128)(2,1)} fusion(bf16[1,3,1024,1024]{3,2,1,0:T(8,128)(2,1)} %param.6, f32[3,1024,128]{1,2,0:T(8,128)S(1)} %reshape.73), kind=kOutput, calls=%fused_computation.20 | convolution fusion | flops 806092800 | bytes 8650752 | tf_op jit(solution)/shard_map/kdr,kdc->krc/dot_general | solution.py:67
  148.8 0.1 copy.35
  149.1 52.7 %all-reduce.2.cloned.1.call-done = bf16[3,1024,128]{1,2,0:T(8,128)(2,1)} async-done(((bf16[3,1024,128]{1,2,0:T(8,128)(2,1)}), bf16[3,1024,128]{1,2,0:T(8,128)(2,1)}) %all-reduce.2.cloned.1.call-update) | async-done | bytes 786448 | tf_op jit(solution)/shard_map/psum | solution.py:72
  201.8 1.4 convert_element_type.64
  203.2 0.2 fusion.28
  203.4 10.0 %all_gather.6 = bf16[3,1024,128]{1,2,0:T(8,128)(2,1)S(1)} all-gather(bf16[3,128,128]{1,2,0:T(8,128)(2,1)S(1)} %get-tuple-element.16), channel_id=1, replica_groups=mesh['dp'=8,'own'=4] {'dp'}, dimensions={1}, use_global_device_ids=true | all-gather | bytes 884736 | tf_op jit(solution)/shard_map/all_gather | solution.py:76
  213.4 0.2 fusion.11
  213.6 0.2 multiply_reduce_fusion
  213.9 5.9 %fusion.13 = bf16[3,1024,128]{1,2,0:T(8,128)(2,1)} fusion(f32[3,1024,128]{1,2,0:T(8,128)S(1)} %reshape.73, bf16[1,3,1024,1024]{3,2,1,0:T(8,128)(2,1)} %param.6, bf16[3,1024,128]{1,2,0:T(8,128)(2,1)S(1)} %all_gather.6, f32[3,128]{1,0:T(4,128)S(1)} %add_divide_fusion, bf16[3,1024,128]{1,2,0:T(8,128)(2,1)S(1)} %copy-done.2), kind=kOutput, calls=%fused_computation.17 | convolution fusion | flops 808452096 | bytes 10225152 | tf_op jit(solution)/shard_map/kdr,krc->kdc/dot_general | solution.py:86
  219.8 45.6 %all-gather.2.cloned.1.call-done = bf16[3,8192,128]{1,2,0:T(8,128)(2,1)} async-done(((bf16[3,1024,128]{1,2,0:T(8,128)(2,1)}), bf16[3,8192,128]{1,2,0:T(8,128)(2,1)}) %all-gather.2.cloned.1.call-update) | async-done | bytes 6291472 | tf_op jit(solution)/shard_map/all_gather | solution.py:90
  265.4 11.1 %reshape.74 = bf16[3,4,2048,128]{2,1,3,0:T(4,128)(2,1)} reshape(bf16[3,8192,128]{1,2,0:T(8,128)(2,1)} %all-gather.2.cloned.1.call-done) | data formatting | bytes 12582912 | tf_op jit(solution)/shard_map/reshape | solution.py:91
  276.5 11.2 %copy.40 = bf16[3,4,2048,128]{3,2,0,1:T(8,128)(2,1)} copy(bf16[3,4,2048,128]{2,1,3,0:T(4,128)(2,1)} %reshape.74) | data formatting | bytes 12582912 | tf_op jit(solution)/shard_map/reshape | solution.py:91
  287.7 5.4 %all-to-all-start.2 = ((bf16[3,4,2048,128]{3,2,0,1:T(8,128)(2,1)}), bf16[3,4,2048,128]{3,2,0,1:T(8,128)(2,1)}, u32[]{:S(2)}, u32[]{:S(2)}) async-start(bf16[3,4,2048,128]{3,2,0,1:T(8,128)(2,1)} %copy.40), calls=%async_computation.3 | async-start | bytes 12582912 | tf_op jit(solution)/shard_map/all_to_all | solution.py:92
  293.1 0.8 copy.43
  293.9 0.8 copy.44
  294.7 137.2 %all-to-all-done.2 = bf16[3,4,2048,128]{3,2,0,1:T(8,128)(2,1)} async-done(((bf16[3,4,2048,128]{3,2,0,1:T(8,128)(2,1)}), bf16[3,4,2048,128]{3,2,0,1:T(8,128)(2,1)}, u32[]{:S(2)}, u32[]{:S(2)}) %all-to-all-start.2) | async-done | bytes 6291488 | tf_op jit(solution)/shard_map/all_to_all | solution.py:92
  431.9 6.7 %fusion.8 = bf16[6,2048,128]{2,0,1:T(8,128)(2,1)S(1)} fusion(bf16[12,2048,128]{2,1,0:T(8,128)(2,1)} %bitcast.15, s32[12]{0:T(128)S(1)} %get-tuple-element.18, s32[12]{0:T(128)S(1)} %get-tuple-element.19, s32[6]{0:T(128)S(1)} %convert_reduce_fusion, s32[6]{0:T(128)S(1)} %copy-done.5), kind=kOutput, calls=%fused_computation.10 | convolution fusion | flops 39321816 | bytes 9437328 | tf_op jit(solution)/shard_map/sj,sdc->jdc/dot_general | solution.py:94
  438.6 2.1 copy.42
  (23 shorter events, 0.4 us)
Async XLA Ops:
  7.2 1.9 copy-start
  7.2 84.2 %reduce-scatter.2.cloned.1.call-start = ((), (), s32[]{:S(2)}) async-start(), calls=%async_computation.4 | async-start | bytes 7077888 | tf_op jit(solution)/shard_map/reduce_scatter | solution.py:49
  91.4 24.6 %all-to-all-start = ((bf16[4,3,256,128]{3,2,1,0:T(8,128)(2,1)}), bf16[4,3,256,128]{3,2,1,0:T(8,128)(2,1)S(1)}, u32[]{:S(2)}, u32[]{:S(2)}) async-start(bf16[4,3,256,128]{3,2,1,0:T(8,128)(2,1)} %bitcast.63), calls=%async_computation.1 | async-start | bytes 1572864 | tf_op jit(solution)/shard_map/all_to_all | solution.py:51
  117.7 24.5 %all-to-all-start.1 = ((bf16[8,3,256,128]{3,2,1,0:T(8,128)(2,1)}), bf16[8,3,256,128]{3,2,1,0:T(8,128)(2,1)S(1)}, u32[]{:S(2)}, u32[]{:S(2)}) async-start(bf16[8,3,256,128]{3,2,1,0:T(8,128)(2,1)} %fusion.7), calls=%async_computation.2 | async-start | bytes 3145728 | tf_op jit(solution)/shard_map/all_to_all | solution.py:58
  121.3 80.5 %all-reduce.2.cloned.1.call-start = ((), (), s32[]{:S(2)}) async-start(), calls=%async_computation.5 | async-start | bytes 1572864 | tf_op jit(solution)/shard_map/psum | solution.py:72
  144.0 4.8 %copy-start.3 = (f32[1,3,128,128]{3,2,1,0:T(8,128)S(1)}, f32[1,3,128,128]{3,2,1,0:T(8,128)}, u32[]{:S(2)}) copy-start(f32[1,3,128,128]{3,2,1,0:T(8,128)} %param.7) | copy-start | bytes 589828
  144.0 4.9 %copy-start.4 = (f32[1,3,128,128]{3,2,1,0:T(8,128)S(1)}, f32[1,3,128,128]{3,2,1,0:T(8,128)}, u32[]{:S(2)}) copy-start(f32[1,3,128,128]{3,2,1,0:T(8,128)} %param.8) | copy-start | bytes 589828
  148.8 116.6 %all-gather.2.cloned.1.call-start = ((), (), s32[]{:S(2)}) async-start(), calls=%async_computation.6 | async-start | bytes 7077888 | tf_op jit(solution)/shard_map/all_gather | solution.py:90
  201.8 11.8 %copy-start.2 = (bf16[3,1024,128]{1,2,0:T(8,128)(2,1)S(1)}, bf16[3,1024,128]{1,2,0:T(8,128)(2,1)}, u32[]{:S(2)}) copy-start(bf16[3,1024,128]{1,2,0:T(8,128)(2,1)} %all-reduce.2.cloned.1.call-done) | copy-start | bytes 2359300
  287.7 144.2 %copy-start.5 = (s32[6]{0:T(128)S(1)}, s32[6]{0:T(128)}, u32[]{:S(2)}) copy-start(s32[6]{0:T(128)} %param.9) | copy-start | bytes 76
  287.7 144.2 %all-to-all-start.2 = ((bf16[3,4,2048,128]{3,2,0,1:T(8,128)(2,1)}), bf16[3,4,2048,128]{3,2,0,1:T(8,128)(2,1)}, u32[]{:S(2)}, u32[]{:S(2)}) async-start(bf16[3,4,2048,128]{3,2,0,1:T(8,128)(2,1)} %copy.40), calls=%async_computation.3 | async-start | bytes 12582912 | tf_op jit(solution)/shard_map/all_to_all | solution.py:92
  431.9 8.7 %copy-start.1 = (bf16[1,6,2048,128]{3,2,1,0:T(8,128)(2,1)S(1)}, bf16[1,6,2048,128]{3,2,1,0:T(8,128)(2,1)}, u32[]{:S(2)}) copy-start(bf16[1,6,2048,128]{3,2,1,0:T(8,128)(2,1)} %param.5) | copy-start | bytes 9437188
Sparse Core Ops, SparseCore 0:
  26.9 64.4 reduce-scatter.1
  148.9 52.8 all-reduce.1
  219.9 45.3 all-gather.1
where the time goes:
time: 448 us; the launch traced here: 447 us
  waiting for transfers between devices  341 us (76%)
  local copies, waits for them, and re-layouts  33.4 us (7%)
  matrix products  30.5 us (7%)
  between operations  13.9 us (3%)
  starting transfers between devices  13.7 us (3%)
  blocking collectives  10 us (2%)
  other arithmetic  4.87 us (1%)
    all_to_all x1, waiting for transfers between devices, local(): lax.all_to_all(gathered, 'own', split_axis=1, concat_axis=0, tiled=True)  137 us
    reduce_scatter x1, waiting for transfers between devices, local(): lax.psum_scatter(blocked, 'dp', scatter_dimension=1, tiled=True)  64.6 us
    psum x1, waiting for transfers between devices, local(): lax.psum(partial_value.astype(jnp.bfloat16), 'dp').astype(jnp.float32)  52.7 us
    all_gather x1, waiting for transfers between devices, local(): gathered = lax.all_gather(update_half, 'dp', axis=1, tiled=True)  45.6 us
    reshape x2, local copies, waits for them, and re-layouts, local(): gathered = gathered.reshape(capacity, owner_count, own_rows, columns)  22.4 us
    all_to_all x1, waiting for transfers between devices, local(): lax.all_to_all(placed.astype(jnp.bfloat16), 'dp', split_axis=0, concat_ax...  20.9 us
    all_to_all x1, waiting for transfers between devices, local(): lax.all_to_all(pieces.astype(jnp.bfloat16), 'own', split_axis=0, concat_a...  19.8 us
    dot_general x1, matrix products, local(): jnp.einsum('sj,jdc->sdc', selector, grads[0], preferred_element_type=jnp....  13.2 us
  transfers between devices with their start and end apart: 6, of which 6 were waited for; matrix products, arithmetic and copies ran while one was open for 0% of the time, Pallas kernels for 0%

commit v1 on v0

--- a/solution.py
+++ b/solution.py
@@ -89,7 +89,10 @@
     update_half = update_full.astype(jnp.bfloat16)
     gathered = lax.all_gather(update_half, "dp", axis=1, tiled=True)
     gathered = gathered.reshape(capacity, owner_count, own_rows, columns)
-    returned = lax.all_to_all(gathered, "own", split_axis=1, concat_axis=0, tiled=True)
+    returned = jnp.concatenate(
+        lax.all_to_all(jnp.stack(jnp.split(gathered, lax.axis_size("own"), axis=1)), "own", 0, 0),
+        axis=0,
+    )
     slot_rows = returned.reshape(owner_count * capacity, own_rows, columns)
     update = jnp.einsum(
         "sj,sdc->jdc", selector, slot_rows, preferred_element_type=jnp.float32

time: 448 us -> 494 us (1.10)
  local copies, waits for them, and re-layouts: 33.4 us -> 72.7 us
  other arithmetic: 4.87 us -> 11.4 us
    unnamed x17 -> x21, local copies, waits for them, and re-layouts: 4.83 us -> 34.6 us
    split x0 -> x1, local copies, waits for them, and re-layouts: none -> 20.8 us  [local(): jnp.split(gathered, lax.axis_size('own'), axis=1)]
    reshape x2 -> x1, local copies, waits for them, and re-layouts: 22.4 us -> 11.1 us  [local(): gathered = gathered.reshape(capacity, owner_count, own_rows, columns)]
    another operation x0 -> x1, other arithmetic: none -> 6.49 us  [local(): jnp.stack(jnp.split(gathered, lax.axis_size('own'), axis=1))]
where the time goes in v1:
time: 494 us; the launch traced here: 493 us
  waiting for transfers between devices  341 us (69%)
  local copies, waits for them, and re-layouts  72.7 us (15%)
  matrix products  30.5 us (6%)
  between operations  13.9 us (3%)
  starting transfers between devices  13.7 us (3%)
  other arithmetic  11.4 us (2%)
  blocking collectives  10 us (2%)
    all_to_all x1, waiting for transfers between devices, local(): lax.all_to_all(jnp.stack(jnp.split(gathered, lax.axis_size('own'), axis=1...  137 us
    reduce_scatter x1, waiting for transfers between devices, local(): lax.psum_scatter(blocked, 'dp', scatter_dimension=1, tiled=True)  64.6 us
    psum x1, waiting for transfers between devices, local(): lax.psum(partial_value.astype(jnp.bfloat16), 'dp').astype(jnp.float32)  52.8 us
    all_gather x1, waiting for transfers between devices, local(): gathered = lax.all_gather(update_half, 'dp', axis=1, tiled=True)  45.6 us
    unnamed x21, local copies, waits for them, and re-layouts  34.6 us
    all_to_all x1, waiting for transfers between devices, local(): lax.all_to_all(placed.astype(jnp.bfloat16), 'dp', split_axis=0, concat_ax...  20.9 us
    split x1, local copies, waits for them, and re-layouts, local(): jnp.split(gathered, lax.axis_size('own'), axis=1)  20.8 us
    all_to_all x1, waiting for transfers between devices, local(): lax.all_to_all(pieces.astype(jnp.bfloat16), 'own', split_axis=0, concat_a...  19.8 us
  transfers between devices with their start and end apart: 6, of which 6 were waited for; matrix products, arithmetic and copies ran while one was open for 0% of the time, Pallas kernels for 0%

profile of v1, /device:TPU:0, one launch (start us, length us, event | category | flops | bytes accessed | tf_op | source)
XLA Modules:
  0.0 493.1 jit_solution(3795367024000019803)
XLA Ops:
  7.2 1.0 convert_reduce_fusion
  8.2 0.8 copy-done
  9.1 13.2 %convolution_convert_fusion = bf16[12,2048,128]{2,0,1:T(8,128)(2,1)S(1)} fusion(bf16[6,2048,128]{2,1,0:T(8,128)(2,1)S(1)} %bitcast.60, s32[12]{0:T(128)S(1)} %get-tuple-element.22, s32[12]{0:T(128)S(1)} %get-tuple-element.23, s32[6]{0:T(128)S(1)} %convert_reduce_fusion, s32[6]{0:T(128)} %param.9), kind=kOutput, calls=%fused_computation.2 | convolution fusion | flops 40894680 | bytes 9437328 | tf_op jit(solution)/shard_map/sj,jdc->sdc/dot_general | solution.py:43
  22.3 4.4 copy.46
  26.8 64.6 %reduce-scatter.2.cloned.1.call-done = bf16[12,1,256,128]{3,2,0,1:T(8,128)(2,1)} async-done(((bf16[12,8,256,128]{3,2,0,1:T(8,128)(2,1)}), bf16[12,1,256,128]{3,2,0,1:T(8,128)(2,1)}) %reduce-scatter.2.cloned.1.call-update) | async-done | bytes 786448 | tf_op jit(solution)/shard_map/reduce_scatter | solution.py:49
  91.4 4.6 all-to-all-start
  96.1 19.8 %all-to-all-done = bf16[4,3,256,128]{3,2,1,0:T(8,128)(2,1)S(1)} async-done(((bf16[4,3,256,128]{3,2,1,0:T(8,128)(2,1)}), bf16[4,3,256,128]{3,2,1,0:T(8,128)(2,1)S(1)}, u32[]{:S(2)}, u32[]{:S(2)}) %all-to-all-start) | async-done | bytes 786464 | tf_op jit(solution)/shard_map/all_to_all | solution.py:51
  116.1 1.6 fusion.7
  117.7 3.6 all-to-all-start.1
  121.3 20.9 %all-to-all-done.1 = bf16[8,3,256,128]{3,2,1,0:T(8,128)(2,1)S(1)} async-done(((bf16[8,3,256,128]{3,2,1,0:T(8,128)(2,1)}), bf16[8,3,256,128]{3,2,1,0:T(8,128)(2,1)S(1)}, u32[]{:S(2)}, u32[]{:S(2)}) %all-to-all-start.1) | async-done | bytes 1572896 | tf_op jit(solution)/shard_map/all_to_all | solution.py:58
  142.4 0.8 copy.47
  143.2 0.8 reshape.69
  144.0 4.7 fusion.19
  149.1 52.8 %all-reduce.2.cloned.1.call-done = bf16[3,1024,128]{1,2,0:T(8,128)(2,1)} async-done(((bf16[3,1024,128]{1,2,0:T(8,128)(2,1)}), bf16[3,1024,128]{1,2,0:T(8,128)(2,1)}) %all-reduce.2.cloned.1.call-update) | async-done | bytes 786448 | tf_op jit(solution)/shard_map/psum | solution.py:72
  201.9 1.4 convert_element_type.64
  203.4 10.0 %all_gather.6 = bf16[3,1024,128]{1,2,0:T(8,128)(2,1)S(1)} all-gather(bf16[3,128,128]{1,2,0:T(8,128)(2,1)S(1)} %get-tuple-element.20), channel_id=1, replica_groups=mesh['dp'=8,'own'=4] {'dp'}, dimensions={1}, use_global_device_ids=true | all-gather | bytes 884736 | tf_op jit(solution)/shard_map/all_gather | solution.py:76
  213.7 0.2 multiply_reduce_fusion
  213.9 5.9 %fusion.13 = bf16[3,1024,128]{1,2,0:T(8,128)(2,1)} fusion(f32[3,1024,128]{1,2,0:T(8,128)S(1)} %reshape.69, bf16[1,3,1024,1024]{3,2,1,0:T(8,128)(2,1)} %param.6, bf16[3,1024,128]{1,2,0:T(8,128)(2,1)S(1)} %all_gather.6, f32[3,128]{1,0:T(4,128)S(1)} %add_divide_fusion, bf16[3,1024,128]{1,2,0:T(8,128)(2,1)S(1)} %copy-done.2), kind=kOutput, calls=%fused_computation.18 | convolution fusion | flops 808452096 | bytes 10225152 | tf_op jit(solution)/shard_map/kdr,krc->kdc/dot_general | solution.py:86
  219.8 45.6 %all-gather.2.cloned.1.call-done = bf16[3,8192,128]{1,2,0:T(8,128)(2,1)} async-done(((bf16[3,1024,128]{1,2,0:T(8,128)(2,1)}), bf16[3,8192,128]{1,2,0:T(8,128)(2,1)}) %all-gather.2.cloned.1.call-update) | async-done | bytes 6291472 | tf_op jit(solution)/shard_map/all_gather | solution.py:90
  265.4 11.1 %reshape.70 = bf16[3,4,2048,128]{2,1,3,0:T(4,128)(2,1)} reshape(bf16[3,8192,128]{1,2,0:T(8,128)(2,1)} %all-gather.2.cloned.1.call-done) | data formatting | bytes 12582912 | tf_op jit(solution)/shard_map/reshape | solution.py:91
  276.5 20.8 %fusion.40 = (bf16[3,1,2048,128]{2,1,3,0:T(2,128)(2,1)}, bf16[3,1,2048,128]{2,1,3,0:T(2,128)(2,1)}, bf16[3,1,2048,128]{2,1,3,0:T(2,128)(2,1)}, bf16[3,1,2048,128]{2,1,3,0:T(2,128)(2,1)S(1)}) fusion(bf16[3,4,2048,128]{2,1,3,0:T(4,128)(2,1)} %reshape.70), kind=kLoop, calls=%fused_computation.52 | loop fusion | bytes 12582912 | tf_op jit(solution)/shard_map/split | solution.py:93
  297.3 8.2 %copy.57 = bf16[3,1,2048,128]{3,2,0,1:T(8,128)(2,1)} copy(bf16[3,1,2048,128]{2,1,3,0:T(2,128)(2,1)} %get-tuple-element.15) | data formatting | bytes 3145728
  305.5 8.2 %copy.59 = bf16[3,1,2048,128]{3,2,0,1:T(8,128)(2,1)} copy(bf16[3,1,2048,128]{2,1,3,0:T(2,128)(2,1)} %get-tuple-element.16) | data formatting | bytes 3145728
  313.7 8.2 %copy.58 = bf16[3,1,2048,128]{3,2,0,1:T(8,128)(2,1)} copy(bf16[3,1,2048,128]{2,1,3,0:T(2,128)(2,1)} %get-tuple-element.17) | data formatting | bytes 3145728
  321.9 5.2 %copy.60 = bf16[3,1,2048,128]{3,2,0,1:T(8,128)(2,1)} copy(bf16[3,1,2048,128]{2,1,3,0:T(2,128)(2,1)S(1)} %get-tuple-element.18) | data formatting | bytes 3145728
  327.1 6.5 %pad_maximum_fusion = bf16[4,3,1,2048,128]{4,3,1,2,0:T(8,128)(2,1)} fusion(bf16[1,3,1,2048,128]{4,3,1,2,0:T(8,128)(2,1)} %bitcast.65, bf16[1,3,1,2048,128]{4,3,1,2,0:T(8,128)(2,1)} %bitcast.63, bf16[1,3,1,2048,128]{4,3,1,2,0:T(8,128)(2,1)} %bitcast.64, bf16[1,3,1,2048,128]{4,3,1,2,0:T(8,128)(2,1)} %bitcast.62), kind=kLoop, calls=%fused_computation.3 | loop fusion | flops 9437184 | bytes 12582912 | tf_op jit(solution)/shard_map/stack | solution.py:93
  333.6 5.4 %all-to-all-start.2 = ((bf16[4,3,1,2048,128]{4,3,1,2,0:T(8,128)(2,1)}), bf16[4,3,1,2048,128]{4,3,1,2,0:T(8,128)(2,1)}, u32[]{:S(2)}, u32[]{:S(2)}) async-start(bf16[4,3,1,2048,128]{4,3,1,2,0:T(8,128)(2,1)} %pad_maximum_fusion), calls=%async_computation.3 | async-start | bytes 12582912 | tf_op jit(solution)/shard_map/all_to_all | solution.py:93
  339.0 0.8 copy.56
  339.8 0.8 copy.55
  340.6 137.2 %all-to-all-done.2 = bf16[4,3,1,2048,128]{4,3,1,2,0:T(8,128)(2,1)} async-done(((bf16[4,3,1,2048,128]{4,3,1,2,0:T(8,128)(2,1)}), bf16[4,3,1,2048,128]{4,3,1,2,0:T(8,128)(2,1)}, u32[]{:S(2)}, u32[]{:S(2)}) %all-to-all-start.2) | async-done | bytes 6291488 | tf_op jit(solution)/shard_map/all_to_all | solution.py:93
  477.8 6.7 %fusion.8 = bf16[6,2048,128]{2,0,1:T(8,128)(2,1)S(1)} fusion(bf16[12,2048,128]{2,1,0:T(8,128)(2,1)} %bitcast.17, s32[12]{0:T(128)S(1)} %get-tuple-element.22, s32[12]{0:T(128)S(1)} %get-tuple-element.23, s32[6]{0:T(128)S(1)} %convert_reduce_fusion, s32[6]{0:T(128)S(1)} %copy-done.5), kind=kOutput, calls=%fused_computation.11 | convolution fusion | flops 39321816 | bytes 9437328 | tf_op jit(solution)/shard_map/sj,sdc->jdc/dot_general | solution.py:97
  484.5 2.1 copy.54
  (28 shorter events, 1.2 us)
Async XLA Ops:
  7.2 1.9 copy-start
  7.2 84.2 %reduce-scatter.2.cloned.1.call-start = ((), (), s32[]{:S(2)}) async-start(), calls=%async_computation.4 | async-start | bytes 7077888 | tf_op jit(solution)/shard_map/reduce_scatter | solution.py:49
  91.4 24.6 %all-to-all-start = ((bf16[4,3,256,128]{3,2,1,0:T(8,128)(2,1)}), bf16[4,3,256,128]{3,2,1,0:T(8,128)(2,1)S(1)}, u32[]{:S(2)}, u32[]{:S(2)}) async-start(bf16[4,3,256,128]{3,2,1,0:T(8,128)(2,1)} %bitcast.67), calls=%async_computation.1 | async-start | bytes 1572864 | tf_op jit(solution)/shard_map/all_to_all | solution.py:51
  117.7 24.5 %all-to-all-start.1 = ((bf16[8,3,256,128]{3,2,1,0:T(8,128)(2,1)}), bf16[8,3,256,128]{3,2,1,0:T(8,128)(2,1)S(1)}, u32[]{:S(2)}, u32[]{:S(2)}) async-start(bf16[8,3,256,128]{3,2,1,0:T(8,128)(2,1)} %fusion.7), calls=%async_computation.2 | async-start | bytes 3145728 | tf_op jit(solution)/shard_map/all_to_all | solution.py:58
  121.3 80.6 %all-reduce.2.cloned.1.call-start = ((), (), s32[]{:S(2)}) async-start(), calls=%async_computation.5 | async-start | bytes 1572864 | tf_op jit(solution)/shard_map/psum | solution.py:72
  144.0 4.8 copy-start.3
  144.0 4.9 %copy-start.4 = (f32[1,3,128,128]{3,2,1,0:T(8,128)S(1)}, f32[1,3,128,128]{3,2,1,0:T(8,128)}, u32[]{:S(2)}) copy-start(f32[1,3,128,128]{3,2,1,0:T(8,128)} %param.8) | copy-start | bytes 589828
  148.8 116.6 %all-gather.2.cloned.1.call-start = ((), (), s32[]{:S(2)}) async-start(), calls=%async_computation.6 | async-start | bytes 7077888 | tf_op jit(solution)/shard_map/all_gather | solution.py:90
  201.9 11.8 %copy-start.2 = (bf16[3,1024,128]{1,2,0:T(8,128)(2,1)S(1)}, bf16[3,1024,128]{1,2,0:T(8,128)(2,1)}, u32[]{:S(2)}) copy-start(bf16[3,1024,128]{1,2,0:T(8,128)(2,1)} %all-reduce.2.cloned.1.call-done) | copy-start | bytes 2359300
  333.6 144.2 %copy-start.5 = (s32[6]{0:T(128)S(1)}, s32[6]{0:T(128)}, u32[]{:S(2)}) copy-start(s32[6]{0:T(128)} %param.9) | copy-start | bytes 76
  333.6 144.2 %all-to-all-start.2 = ((bf16[4,3,1,2048,128]{4,3,1,2,0:T(8,128)(2,1)}), bf16[4,3,1,2048,128]{4,3,1,2,0:T(8,128)(2,1)}, u32[]{:S(2)}, u32[]{:S(2)}) async-start(bf16[4,3,1,2048,128]{4,3,1,2,0:T(8,128)(2,1)} %pad_maximum_fusion), calls=%async_computation.3 | async-start | bytes 12582912 | tf_op jit(solution)/shard_map/all_to_all | solution.py:93
  477.8 8.8 %copy-start.1 = (bf16[1,6,2048,128]{3,2,1,0:T(8,128)(2,1)S(1)}, bf16[1,6,2048,128]{3,2,1,0:T(8,128)(2,1)}, u32[]{:S(2)}) copy-start(bf16[1,6,2048,128]{3,2,1,0:T(8,128)(2,1)} %param.5) | copy-start | bytes 9437188
Sparse Core Ops, SparseCore 0:
  26.9 64.4 reduce-scatter.1
  148.9 52.9 all-reduce.1
  220.0 45.3 all-gather.1
